TPU v7x, 512 devices: a whole 4x8x8 slice. The times are simulated.
512 devices in a mesh: af: 32 (over z_hi, x, core), ta: 16 (over y, z_lo).
Axes of the slice: x: 4, y: 8, z: 8 (z_hi: 4, z_lo: 2; z = z_hi * 2 + z_lo), core: 2. Of those that a mesh axis runs over, the one named last changes fastest.
Arguments:
- samples: bfloat16 [4096, 512, 512], P('ta', 'af'), may hold values from -6 to 6
Outputs:
- visibility: float32 [512, 128, 512], P('ta', 'af')
All inputs are finite; a program needn't handle non-finite values.
Results may differ from a plain program's by a relative error of at most 0.0022.
Values may be sent and summed in bfloat16 or wider, within the bound.
A program may use at most 64 MiB of HBM per device.

v0:
```python
import math

import jax
import jax.numpy as jnp
from jax import lax
from jax.sharding import PartitionSpec as P

CH = 128
TAPS = 4


def passed_along(value, axis, steps):
    count = lax.axis_size(axis)
    first, last = (max(0, -steps), min(count, count - steps))
    return lax.ppermute(value, axis, [(source, source + steps) for source in range(first, last)])


def tap_window(taps, samp_len):
    points = jnp.arange(taps * samp_len).astype(jnp.float32)
    centre = (taps * samp_len - 1) / 2.0
    shape_part = jnp.sinc((points - centre) / samp_len)
    taper = jnp.square(jnp.sin(math.pi * (points + 0.5) / (taps * samp_len)))
    return (shape_part * taper).reshape(taps, samp_len)


def dft_table(samp_len, channels):
    sample_idx = jnp.arange(samp_len)[:, None]
    chan_idx = jnp.arange(channels)[None, :]
    phase = (sample_idx * chan_idx % samp_len).astype(jnp.float32) * (2.0 * math.pi / samp_len)
    scale = 1.0 / math.sqrt(samp_len)
    both = jnp.stack([jnp.cos(phase) * scale, -jnp.sin(phase) * scale], axis=2)
    return both.reshape(samp_len, 2 * channels).astype(jnp.bfloat16)


def on_device(samples):
    frames, inputs, samp_len = samples.shape
    earlier = passed_along(samples[frames - (TAPS - 1) :], "ta", 1)
    extended = jnp.concatenate([earlier, samples], axis=0)
    weights = tap_window(TAPS, samp_len)
    filtered = jnp.zeros((frames, inputs, samp_len), jnp.float32)
    for tap in range(TAPS):
        filtered = filtered + weights[tap][None, None, :] * extended[tap : tap + frames].astype(
            jnp.float32
        )
    filtered = filtered.astype(jnp.bfloat16)
    table = dft_table(samp_len, CH)
    spectrum = jnp.einsum("nc,fin->cfi", table, filtered, preferred_element_type=jnp.float32)
    spectrum = spectrum.astype(jnp.bfloat16)
    turned = lax.all_to_all(spectrum, "af", split_axis=0, concat_axis=2, tiled=True)
    all_inputs = turned.shape[2]
    local_chans = turned.shape[0] // 2
    total_frames = frames * lax.axis_size("ta")
    lefts = []
    rotated = []
    for channel in range(local_chans):
        real_part = turned[2 * channel]
        imag_part = turned[2 * channel + 1]
        lefts.append(jnp.concatenate([real_part, imag_part], axis=0))
        rotated.append(jnp.concatenate([imag_part, -real_part], axis=0))
    row_idx = jnp.arange(all_inputs)[:, None]
    col_idx = jnp.arange(all_inputs)[None, :]
    upper = row_idx <= col_idx
    results = []
    for channel in range(local_chans):
        left_rows = lefts[channel]
        turn_rows = rotated[channel]
        stacked = jnp.concatenate([left_rows, turn_rows], axis=1)
        product = lax.dot_general(
            stacked, lefts[channel], (((0,), (0,)), ((), ())), preferred_element_type=jnp.float32
        )
        packed = jnp.where(upper, product[:all_inputs], product[all_inputs:]) / total_frames
        results.append(packed)
    return lax.psum_scatter(jnp.stack(results, axis=1), "ta", scatter_dimension=0, tiled=True)


def solution(mesh):
    in_specs = (P("ta", "af", None),)
    out_specs = P("ta", "af", None)
    return jax.shard_map(
        on_device, mesh=mesh, in_specs=in_specs, out_specs=out_specs, check_vma=False
    )
```

profile of v0, /device:TPU:1, one launch (start us, length us, event | category | flops | bytes accessed | tf_op | source)
XLA Modules:
  0.0 203.4 jit_solution(18428137694564976102)
XLA Ops:
  6.5 0.0 reduce-scatter.2.cloned.1.call-start
  6.5 0.8 slice.85
  7.3 4.8 %collective-permute-start = (bf16[3,16,512]{2,1,0:T(8,128)(2,1)S(1)}, bf16[3,16,512]{2,1,0:T(8,128)(2,1)S(1)}, u32[]{:S(2)}, u32[]{:S(2)}) collective-permute-start(bf16[3,16,512]{2,1,0:T(8,128)(2,1)S(1)} %slice.85), channel_id=1, source_target_pairs={{0,1},{1,2},{2,3},{3,4},{4,5},{5,6},{6,7},{7,8},{8,9},{9,10},{10,1... | collective-permute-start | bytes 147464 | tf_op jit(solution)/shard_map/ppermute | solution.py:15
  12.2 0.1 fusion.67
  12.2 1.1 multiply_convert_fusion
  13.4 0.2 copy.16
  13.6 0.1 reshape.108
  13.7 0.0 collective-permute-done
  13.7 0.0 copy-start
  13.7 3.1 %constant_dynamic-update-slice_fusion = bf16[259,16,512]{2,1,0:T(8,128)(2,1)S(1)} fusion(bf16[259,16,512]{2,1,0:T(8,128)(2,1)S(1)} %constant_dynamic-update-slice_fusion.1, bf16[256,16,512]{2,1,0:T(8,128)(2,1)} %param.1), kind=kLoop, calls=%fused_computation.98 | loop fusion | bytes 8388608 | tf_op jit(solution)/shard_map/concatenate | solution.py:38
  16.8 0.4 copy-done
  17.2 4.5 %add_convert_fusion = bf16[256,16,512]{2,1,0:T(8,128)(2,1)S(1)} fusion(bf16[256,16,512]{2,1,0:T(8,128)(2,1)S(1)} %copy-done, bf16[259,16,512]{2,1,0:T(8,128)(2,1)S(1)} %constant_dynamic-update-slice_fusion, f32[512]{0:T(512)S(1)} %get-tuple-element.14, f32[512]{0:T(512)S(1)} %get-tuple-element.15, f32[512]{0:T(512)S(1)} %get-tuple-element.16, ...), kind=kLoop, calls=%fused_computation | loop fusion | flops 25165824 | bytes 20979712 | tf_op jit(solution)/shard_map/convert_element_type | solution.py:45
  21.7 2.9 %fusion.2 = bf16[256,256,16]{1,0,2:T(8,128)(2,1)S(1)} fusion(bf16[512,256,1]{0,1,2:T(8,128)(2,1)S(1)} %reshape.108, bf16[256,16,512]{2,1,0:T(8,128)(2,1)S(1)} %add_convert_fusion), kind=kOutput, calls=%fused_computation.4 | convolution fusion | flops 1074790400 | bytes 6553600 | tf_op jit(solution)/shard_map/nc,fin->cfi/dot_general | solution.py:47
  24.6 1.2 copy.18
  25.8 54.1 %all_to_all.15 = bf16[256,256,16]{1,2,0:T(8,128)(2,1)S(1)} all-to-all(bf16[256,256,16]{1,2,0:T(8,128)(2,1)S(1)} %copy.18), channel_id=1, replica_groups=mesh['af'=32,'ta'=16] {'af'}, dimensions={0} | all-to-all | bytes 4194304 | tf_op jit(solution)/shard_map/all_to_all | solution.py:49
  79.9 0.2 fusion.80
  80.2 0.7 fusion.13
  80.9 0.1 fusion.12
  81.1 0.7 fusion.21
  81.8 0.1 fusion.10
  82.0 0.7 fusion.29
  82.7 0.1 fusion.8
  82.9 0.7 fusion.37
  83.7 0.1 fusion.6
  83.8 2.4 %pad_maximum_fusion = f32[512,4,512]{2,0,1:T(8,128)} fusion(f32[512,1,512]{2,0,1:T(8,128)S(1)} %fusion.6, f32[512,1,512]{2,0,1:T(8,128)S(1)} %fusion.8, f32[512,1,512]{2,0,1:T(8,128)S(1)} %fusion.10, f32[512,1,512]{2,0,1:T(8,128)S(1)} %fusion.12), kind=kLoop, calls=%fused_computation.1 | loop fusion | flops 3145728 | bytes 8388608 | tf_op jit(solution)/shard_map/stack | solution.py:73
  86.2 0.0 reduce-scatter.2.cloned.1.call-update
  86.2 108.5 %reduce-scatter.2.cloned.1.call-done = f32[32,4,512]{2,0,1:T(8,128)} async-done(((f32[512,4,512]{2,0,1:T(8,128)}), f32[32,4,512]{2,0,1:T(8,128)}) %reduce-scatter.2.cloned.1.call-update) | async-done | bytes 262160 | tf_op jit(solution)/shard_map/reduce_scatter | solution.py:73
  194.7 1.8 copy.19
  (7 shorter events, 0.2 us)
Async XLA Ops:
  6.5 188.2 %reduce-scatter.2.cloned.1.call-start = ((), (), s32[]{:S(2)}) async-start(), calls=%async_computation.2 | async-start | bytes 4456448 | tf_op jit(solution)/shard_map/reduce_scatter | solution.py:73
  7.3 6.3 %collective-permute-start = (bf16[3,16,512]{2,1,0:T(8,128)(2,1)S(1)}, bf16[3,16,512]{2,1,0:T(8,128)(2,1)S(1)}, u32[]{:S(2)}, u32[]{:S(2)}) collective-permute-start(bf16[3,16,512]{2,1,0:T(8,128)(2,1)S(1)} %slice.85), channel_id=1, source_target_pairs={{0,1},{1,2},{2,3},{3,4},{4,5},{5,6},{6,7},{7,8},{8,9},{9,10},{10,1... | collective-permute-start | bytes 147464 | tf_op jit(solution)/shard_map/ppermute | solution.py:15
  13.7 3.5 %copy-start = (bf16[256,16,512]{2,1,0:T(8,128)(2,1)S(1)}, bf16[256,16,512]{2,1,0:T(8,128)(2,1)}, u32[]{:S(2)}) copy-start(bf16[256,16,512]{2,1,0:T(8,128)(2,1)} %param.1) | copy-start | bytes 12582916
Sparse Core Ops, SparseCore 0:
  86.3 108.3 reduce-scatter.1
where the time goes:
time: 206 us; the launch traced here: 203 us
  waiting for transfers between devices  109 us (53%)
  blocking collectives  54.1 us (26%)
  between operations  13.6 us (7%)
  other arithmetic  8.78 us (4%)
  local copies, waits for them, and re-layouts  7.75 us (4%)
  matrix products  5.85 us (3%)
  starting transfers between devices  4.81 us (2%)
    reduce_scatter x1, waiting for transfers between devices, on_device(): lax.psum_scatter(jnp.stack(results, axis=1), 'ta', scatter_dimension=0, t...  108 us
    all_to_all x1, blocking collectives, on_device(): lax.all_to_all(spectrum, 'af', split_axis=0, concat_axis=2, tiled=True)  54.1 us
    ppermute x1, starting transfers between devices, passed_along(): lax.ppermute(value, axis, [(source, source + steps) for source in range(f...  4.8 us
    convert_element_type x1, other arithmetic, on_device(): filtered = filtered.astype(jnp.bfloat16)  4.52 us
  transfers between devices with their start and end apart: 2, of which 1 were waited for; matrix products, arithmetic and copies ran while one was open for 1% of the time, Pallas kernels for 0%

commit v1 on v0

v1 whole, which is shorter than its diff:
```python
import functools
import math

import jax
import jax.numpy as jnp
import numpy as np
from jax import lax
from jax.experimental import pallas as pl
from jax.experimental.pallas import tpu as pltpu
from jax.sharding import PartitionSpec as P

CH = 128
TAPS = 4
MESH = pl.DeviceIdType.MESH
NX, NZ, NY, NCORE = 4, 8, 8, 2
PEERS = NX * NZ * NCORE
STAGES = 2


def tap_window(taps, samp_len):
    points = np.arange(taps * samp_len).astype(np.float64)
    centre = (taps * samp_len - 1) / 2.0
    shape_part = np.sinc((points - centre) / samp_len)
    taper = np.square(np.sin(math.pi * (points + 0.5) / (taps * samp_len)))
    return (shape_part * taper).reshape(taps, samp_len).astype(np.float32)


def dft_table(samp_len, channels):
    sample_idx = np.arange(samp_len)[:, None]
    chan_idx = np.arange(channels)[None, :]
    phase = (sample_idx * chan_idx % samp_len) * (2.0 * math.pi / samp_len)
    scale = 1.0 / math.sqrt(samp_len)
    both = np.stack([np.cos(phase) * scale, -np.sin(phase) * scale], axis=2)
    both = both.reshape(samp_len, channels // STAGES, STAGES, 2)
    both = both.transpose(0, 2, 1, 3)
    return both.reshape(samp_len, 2 * channels).astype(jnp.bfloat16)


def place():
    af, ta = lax.axis_index("af"), lax.axis_index("ta")
    return af // 8 * 2 + ta % 2, af // 2 % NX, af % 2, ta // 2


def turn_peer(step):
    z, x, core, y = place()
    turn = step % NZ
    ahead = jnp.where(turn % 2 == 1, (turn + 1) // 2, NZ - turn // 2)
    z = (z + ahead) % NZ
    rest = step // NZ
    x = (x + rest // NCORE) % NX
    core = (core + rest % NCORE) % NCORE
    return z // 2 * 8 + x * 2 + core, y * 2 + z % 2, z % 2


def correlate_kernel(
    spec_ref, out_ref, held, part, gathered, total, finals,
    turn_send, turn_recv, row_send, row_recv, swap_send, swap_recv,
):
    z, x, core, y = place()
    af, ta = lax.axis_index("af"), lax.axis_index("ta")
    z_lo = z % 2
    inputs, frames = spec_ref.shape[3], spec_ref.shape[4]
    all_inputs = held.shape[2]
    rows = all_inputs // NY
    half = rows // 2

    barrier = pltpu.get_barrier_semaphore()

    @pl.loop(1, PEERS)
    def _(step):
        to_af, to_ta, _ = turn_peer(step)
        pl.semaphore_signal(
            barrier, inc=1, device_id={"af": to_af, "ta": to_ta}, device_id_type=MESH
        )

    @pl.loop(1, NY)
    def _(step):
        to_ta = (y + step) % NY * 2 + z_lo
        pl.semaphore_signal(
            barrier, inc=1, device_id={"af": af, "ta": to_ta}, device_id_type=MESH
        )

    pl.semaphore_wait(barrier, PEERS - 1 + NY - 1)

    my_rows = pl.ds(pl.multiple_of(af * inputs, inputs), inputs)
    my_frames = pl.ds(pl.multiple_of(z_lo * frames, frames), frames)
    for stage in range(STAGES):
        pltpu.make_async_copy(
            spec_ref.at[stage, af * 2 + z_lo],
            held.at[stage, :, my_rows, my_frames],
            turn_recv.at[stage],
        ).start()

        @pl.loop(1, PEERS)
        def _(step):
            to_af, to_ta, to_lo = turn_peer(step)
            pltpu.make_async_remote_copy(
                src_ref=spec_ref.at[stage, to_af * 2 + to_lo],
                dst_ref=held.at[stage, :, my_rows, my_frames],
                send_sem=turn_send.at[stage],
                recv_sem=turn_recv.at[stage],
                device_id={"af": to_af, "ta": to_ta},
                device_id_type=MESH,
            ).start()

    nt = (((1,), (1,)), ((), ()))

    def dot(a, b):
        return lax.dot_general(a, b, nt, preferred_element_type=jnp.float32)

    side = all_inputs // 2
    row_idx = lax.broadcasted_iota(jnp.int32, (side, side), 0)
    col_idx = lax.broadcasted_iota(jnp.int32, (side, side), 1)
    upper = row_idx <= col_idx
    lo, hi = pl.ds(0, side), pl.ds(side, side)

    def send_rows(stage, first, last):
        @pl.loop(first, last)
        def _(to_y):
            block = pl.ds(pl.multiple_of(to_y * rows, rows), rows)

            @pl.when(to_y != y)
            def _():
                pltpu.make_async_remote_copy(
                    src_ref=part.at[stage, block],
                    dst_ref=gathered.at[stage, y],
                    send_sem=row_send.at[stage],
                    recv_sem=row_recv.at[stage],
                    device_id={"af": af, "ta": to_y * 2 + z_lo},
                    device_id_type=MESH,
                ).start()

            @pl.when(to_y == y)
            def _():
                pltpu.make_async_copy(
                    part.at[stage, block], gathered.at[stage, y], row_recv.at[stage]
                ).start()

    for stage in range(STAGES):
        pltpu.make_async_copy(held.at[stage], held.at[stage], turn_recv.at[stage]).wait()
        for own, other in ((lo, hi), (hi, lo)):
            a, b = held[stage, 0, own], held[stage, 1, own]
            c, d = held[stage, 0, other], held[stage, 1, other]
            real = dot(a, a) + dot(b, b)
            imag = dot(b, a) - dot(a, b)
            part[stage, own, own] = jnp.where(upper, real, imag).astype(part.dtype)
            if own is lo:
                part[stage, own, other] = (dot(a, c) + dot(b, d)).astype(part.dtype)
                send_rows(stage, 0, NY // 2)
            else:
                part[stage, own, other] = (dot(b, c) - dot(a, d)).astype(part.dtype)
                send_rows(stage, NY // 2, NY)

    scale = 1.0 / (frames * lax.axis_size("ta"))
    own_half = pl.ds(pl.multiple_of(z_lo * half, half), half)
    other_half = pl.ds(pl.multiple_of((1 - z_lo) * half, half), half)
    for stage in range(STAGES):
        pltpu.make_async_copy(
            gathered.at[stage], gathered.at[stage], row_recv.at[stage]
        ).wait()
        acc = gathered[stage, 0].astype(jnp.float32)
        for k in range(1, NY):
            acc = acc + gathered[stage, k].astype(jnp.float32)
        total[stage] = acc * scale
        pltpu.make_async_remote_copy(
            src_ref=total.at[stage, other_half],
            dst_ref=finals.at[z_lo * STAGES + stage],
            send_sem=swap_send.at[stage],
            recv_sem=swap_recv.at[stage],
            device_id={"af": af, "ta": y * 2 + 1 - z_lo},
            device_id_type=MESH,
        ).start()
        pltpu.make_async_copy(
            total.at[stage, own_half],
            finals.at[z_lo * STAGES + stage],
            swap_recv.at[stage],
        ).start()

    for stage in range(STAGES):
        both = finals.at[pl.ds(0, 2)]
        pltpu.make_async_copy(both, both, swap_recv.at[stage]).wait()
    for k in range(2 * STAGES):
        out_ref[:, k, :] = finals[k]

    for stage in range(STAGES):
        sent = spec_ref.at[stage, pl.ds(0, PEERS - 1)]
        pltpu.make_async_copy(sent, sent, turn_send.at[stage]).wait()
        sent = gathered.at[stage, pl.ds(0, NY - 1)]
        pltpu.make_async_copy(sent, sent, row_send.at[stage]).wait()
        sent = finals.at[0]
        pltpu.make_async_copy(sent, sent, swap_send.at[stage]).wait()


def correlate(spectrum):
    _, _, _, inputs, frames = spectrum.shape
    all_inputs = inputs * lax.axis_size("af")
    rows = all_inputs // NY
    dma = pltpu.SemaphoreType.DMA
    return pl.pallas_call(
        correlate_kernel,
        out_shape=jax.ShapeDtypeStruct((rows // 2, 2 * STAGES, all_inputs), jnp.float32),
        in_specs=[pl.BlockSpec(memory_space=pltpu.VMEM)],
        out_specs=pl.BlockSpec(memory_space=pltpu.VMEM),
        scratch_shapes=[
            pltpu.VMEM((STAGES, 2, all_inputs, 2 * frames), jnp.bfloat16),
            pltpu.VMEM((STAGES, all_inputs, all_inputs), jnp.bfloat16),
            pltpu.VMEM((STAGES, NY, rows, all_inputs), jnp.bfloat16),
            pltpu.VMEM((STAGES, rows, all_inputs), jnp.float32),
            pltpu.VMEM((2 * STAGES, rows // 2, all_inputs), jnp.float32),
            dma((STAGES,)), dma((STAGES,)), dma((STAGES,)),
            dma((STAGES,)), dma((STAGES,)), dma((STAGES,)),
        ],
        compiler_params=pltpu.CompilerParams(
            collective_id=0, has_side_effects=True, vmem_limit_bytes=48 * 2**20
        ),
    )(spectrum)


def passed_along(value, axis, steps):
    count = lax.axis_size(axis)
    first, last = (max(0, -steps), min(count, count - steps))
    return lax.ppermute(value, axis, [(source, source + steps) for source in range(first, last)])


def filtered_by(weights, extended, frames):
    total = jnp.zeros((frames,) + extended.shape[1:], jnp.float32)
    for tap in range(TAPS):
        total = total + weights[tap][None, None, :] * extended[tap : tap + frames].astype(
            jnp.float32
        )
    return total.astype(jnp.bfloat16)


def on_device(samples):
    frames, inputs, samp_len = samples.shape
    weights = jnp.asarray(tap_window(TAPS, samp_len))
    halo = TAPS - 1
    earlier = passed_along(samples[frames - halo :], "ta", 1)
    padded = jnp.pad(samples, ((halo, 0), (0, 0), (0, 0)))
    filtered = filtered_by(weights, padded, frames)
    first = filtered_by(weights, jnp.concatenate([earlier, samples[:halo]], axis=0), halo)
    filtered = lax.dynamic_update_slice(filtered, first, (0, 0, 0))
    table = jnp.asarray(dft_table(samp_len, CH))
    spectrum = jnp.einsum("nc,fin->cif", table, filtered, preferred_element_type=jnp.float32)
    spectrum = spectrum.astype(jnp.bfloat16)
    spectrum = spectrum.reshape(STAGES, PEERS, 2, inputs, frames)
    return correlate(spectrum)


def solution(mesh):
    in_specs = (P("ta", "af", None),)
    out_specs = P("ta", "af", None)
    return jax.shard_map(
        on_device, mesh=mesh, in_specs=in_specs, out_specs=out_specs, check_vma=False
    )
```

time: 206 us -> 102 us (0.50)
  the two profiles are of different devices: /device:TPU:1 before, /device:TPU:56 now
where the time goes in v1:
time: 102 us; the launch traced here: 101 us
  Pallas kernels  83.2 us (82%)
  other arithmetic  7.91 us (8%)
  starting transfers between devices  4.41 us (4%)
  matrix products  2.92 us (3%)
  local copies, waits for them, and re-layouts  2.76 us (3%)
    pallas_call x1, Pallas kernels, correlate(): pl.pallas_call(correlate_kernel, out_shape=jax.ShapeDtypeStruct((rows //...  83.2 us
    convert_element_type x1, other arithmetic, filtered_by(): return total.astype(jnp.bfloat16)  7.87 us
    ppermute x1, starting transfers between devices, passed_along(): lax.ppermute(value, axis, [(source, source + steps) for source in range(f...  4.41 us
    dot_general x1, matrix products, on_device(): jnp.einsum('nc,fin->cif', table, filtered, preferred_element_type=jnp.flo...  2.92 us
  transfers between devices with their start and end apart: 1, of which 0 were waited for; matrix products, arithmetic and copies ran while one was open for 8% of the time, Pallas kernels for 0%

profile of v1, /device:TPU:56, one launch (start us, length us, event | category | flops | bytes accessed | tf_op | source)
XLA Modules:
  0.0 101.3 jit_solution(12321737464580245220)
XLA Ops:
  0.0 0.8 fusion.6
  0.8 0.0 copy-start
  0.8 0.0 copy-start.1
  0.8 0.0 copy-start.2
  0.9 0.0 copy-start.3
  0.9 0.0 copy-start.4
  0.9 4.4 %collective-permute-start = (bf16[3,16,512]{2,1,0:T(8,128)(2,1)S(1)}, bf16[3,16,512]{2,1,0:T(8,128)(2,1)S(1)}, u32[]{:S(2)}, u32[]{:S(2)}) collective-permute-start(bf16[3,16,512]{2,1,0:T(8,128)(2,1)S(1)} %get-tuple-element.5), channel_id=1, source_target_pairs={{0,1},{1,2},{2,3},{3,4},{4,5},{5,6},{6,7},{7,8},{8,9},{9,10},{10,1... | collective-permute-start | bytes 147464 | tf_op jit(solution)/shard_map/ppermute | solution.py:222
  5.3 7.9 %add_convert_fusion = bf16[256,16,512]{2,1,0:T(8,128)(2,1)S(1)} fusion(bf16[256,16,512]{2,1,0:T(8,128)(2,1)} %param.3, f32[512]{0:T(512)} %constant.20, f32[512]{0:T(512)} %constant.18, f32[512]{0:T(512)} %constant.16, f32[512]{0:T(512)} %constant.14), kind=kLoop, calls=%fused_computation | loop fusion | flops 25165824 | bytes 8396800 | tf_op jit(solution)/shard_map/convert_element_type | solution.py:231
  13.2 0.0 collective-permute-done
  13.2 0.0 copy-done
  13.2 0.0 copy-done.1
  13.2 0.0 copy-done.2
  13.2 0.0 copy-done.3
  13.3 0.0 copy-done.4
  13.3 2.9 %convert_bitcast_fusion = bf16[256,16,256]{2,0,1:T(8,128)(2,1)S(1)} fusion(bf16[512,256,1]{0,1,2:T(8,128)(2,1)S(1)} %copy-done.4, bf16[256,16,512]{2,1,0:T(8,128)(2,1)S(1)} %fusion.4), kind=kOutput, calls=%fused_computation.4 | convolution fusion | flops 1074790400 | bytes 6553600 | tf_op jit(solution)/shard_map/nc,fin->cif/dot_general | solution.py:244
  16.2 1.2 %copy.5 = bf16[256,16,256]{2,1,0:T(8,128)(2,1)S(1)} copy(bf16[256,16,256]{2,0,1:T(8,128)(2,1)S(1)} %convert_bitcast_fusion) | data formatting | bytes 4194304 | tf_op jit(solution)/shard_map/convert_element_type | solution.py:245
  17.4 83.2 %shard_map.37 = f32[32,4,512]{2,1,0:T(4,128)S(1)} custom-call(bf16[2,64,2,16,256]{4,3,2,1,0:T(8,128)(2,1)S(1)} %bitcast.5), custom_call_target="tpu_custom_call" | custom-call | tf_op jit(solution)/shard_map/pallas_call | solution.py:199
  100.6 0.7 copy.12
  (1 shorter events, 0.0 us)
Async XLA Ops:
  0.8 12.4 %copy-start = (f32[512]{0:T(512)S(1)}, f32[512]{0:T(512)}, u32[]{:S(2)}) copy-start(f32[512]{0:T(512)} %constant.20) | copy-start | bytes 6148
  0.8 12.4 %copy-start.1 = (f32[512]{0:T(512)S(1)}, f32[512]{0:T(512)}, u32[]{:S(2)}) copy-start(f32[512]{0:T(512)} %constant.18) | copy-start | bytes 6148
  0.8 12.4 %copy-start.2 = (f32[512]{0:T(512)S(1)}, f32[512]{0:T(512)}, u32[]{:S(2)}) copy-start(f32[512]{0:T(512)} %constant.16) | copy-start | bytes 6148
  0.9 12.4 %copy-start.3 = (f32[512]{0:T(512)S(1)}, f32[512]{0:T(512)}, u32[]{:S(2)}) copy-start(f32[512]{0:T(512)} %constant.14) | copy-start | bytes 6148
  0.9 12.4 %copy-start.4 = (bf16[512,256,1]{0,1,2:T(8,128)(2,1)S(1)}, bf16[512,256,1]{0,1,2:T(8,128)(2,1)}, u32[]{:S(2)}) copy-start(bf16[512,256,1]{0,1,2:T(8,128)(2,1)} %constant.21) | copy-start | bytes 786436
  0.9 12.3 %collective-permute-start = (bf16[3,16,512]{2,1,0:T(8,128)(2,1)S(1)}, bf16[3,16,512]{2,1,0:T(8,128)(2,1)S(1)}, u32[]{:S(2)}, u32[]{:S(2)}) collective-permute-start(bf16[3,16,512]{2,1,0:T(8,128)(2,1)S(1)} %get-tuple-element.5), channel_id=1, source_target_pairs={{0,1},{1,2},{2,3},{3,4},{4,5},{5,6},{6,7},{7,8},{8,9},{9,10},{10,1... | collective-permute-start | bytes 147464 | tf_op jit(solution)/shard_map/ppermute | solution.py:222

commit v2 on v1

--- a/solution.py
+++ b/solution.py
@@ -15,6 +15,8 @@
 NX, NZ, NY, NCORE = 4, 8, 8, 2
 PEERS = NX * NZ * NCORE
 STAGES = 2
+CHUNKS = 2
+BLOCK = 16
 
 
 def tap_window(taps, samp_len):
@@ -38,70 +40,160 @@
 
 def place():
     af, ta = lax.axis_index("af"), lax.axis_index("ta")
-    return af // 8 * 2 + ta % 2, af // 2 % NX, af % 2, ta // 2
+    z = lax.div(af, 8) * 2 + lax.rem(ta, 2)
+    return z, lax.rem(lax.div(af, 2), NX), lax.rem(af, 2), lax.div(ta, 2)
 
 
 def turn_peer(step):
     z, x, core, y = place()
-    turn = step % NZ
-    ahead = jnp.where(turn % 2 == 1, (turn + 1) // 2, NZ - turn // 2)
-    z = (z + ahead) % NZ
-    rest = step // NZ
-    x = (x + rest // NCORE) % NX
-    core = (core + rest % NCORE) % NCORE
-    return z // 2 * 8 + x * 2 + core, y * 2 + z % 2, z % 2
+    turn, rest = lax.rem(step, NZ), lax.div(step, NZ)
+    odd = lax.rem(turn, 2)
+    hop = lax.div(turn + 1, 2)
+    z = lax.rem(z + odd * hop + (1 - odd) * (NZ - hop), NZ)
+    x = lax.rem(x + lax.div(rest, NCORE), NX)
+    core = lax.rem(core + rest, NCORE)
+    z_lo = lax.rem(z, 2)
+    return lax.div(z, 2) * 8 + x * 2 + core, y * 2 + z_lo, z_lo
 
 
 def correlate_kernel(
-    spec_ref, out_ref, held, part, gathered, total, finals,
+    x_hbm, w_hbm, t_hbm, out_ref,
+    window, table, samples, halo, filtered, spectra, turned, spec,
+    held, part, gathered, total, finals,
+    load_sem, halo_send, halo_recv,
     turn_send, turn_recv, row_send, row_recv, swap_send, swap_recv,
 ):
     z, x, core, y = place()
     af, ta = lax.axis_index("af"), lax.axis_index("ta")
-    z_lo = z % 2
-    inputs, frames = spec_ref.shape[3], spec_ref.shape[4]
+    z_lo = lax.rem(z, 2)
+    n_ta = lax.axis_size("ta")
+    frames, inputs, samp_len = x_hbm.shape
+    edge = TAPS - 1
+    chunk = frames // CHUNKS
     all_inputs = held.shape[2]
     rows = all_inputs // NY
     half = rows // 2
 
+    loads = [
+        pltpu.make_async_copy(w_hbm, window, load_sem.at[0]),
+        pltpu.make_async_copy(t_hbm, table, load_sem.at[1]),
+        pltpu.make_async_copy(
+            x_hbm.at[pl.ds(chunk - edge, chunk + edge)],
+            samples.at[pl.ds(chunk, chunk + edge)],
+            load_sem.at[2],
+        ),
+        pltpu.make_async_copy(
+            x_hbm.at[pl.ds(0, chunk - edge)],
+            samples.at[pl.ds(edge, chunk - edge)],
+            load_sem.at[3],
+        ),
+    ]
+    for load in loads:
+        load.start()
+
     barrier = pltpu.get_barrier_semaphore()
+
+    def greet(to_af, to_ta):
+        pl.semaphore_signal(
+            barrier, inc=1, device_id={"af": to_af, "ta": to_ta}, device_id_type=MESH
+        )
 
     @pl.loop(1, PEERS)
     def _(step):
         to_af, to_ta, _ = turn_peer(step)
-        pl.semaphore_signal(
-            barrier, inc=1, device_id={"af": to_af, "ta": to_ta}, device_id_type=MESH
-        )
+        greet(to_af, to_ta)
 
     @pl.loop(1, NY)
     def _(step):
-        to_ta = (y + step) % NY * 2 + z_lo
-        pl.semaphore_signal(
-            barrier, inc=1, device_id={"af": af, "ta": to_ta}, device_id_type=MESH
-        )
-
-    pl.semaphore_wait(barrier, PEERS - 1 + NY - 1)
+        greet(af, lax.rem(y + step, NY) * 2 + z_lo)
+
+    after, before = lax.rem(ta + 1, n_ta), lax.rem(ta + n_ta - 1, n_ta)
+    greet(af, after)
+    greet(af, before)
+    n_greet = PEERS - 1 + NY - 1 + 2
 
     my_rows = pl.ds(pl.multiple_of(af * inputs, inputs), inputs)
-    my_frames = pl.ds(pl.multiple_of(z_lo * frames, frames), frames)
-    for stage in range(STAGES):
-        pltpu.make_async_copy(
-            spec_ref.at[stage, af * 2 + z_lo],
-            held.at[stage, :, my_rows, my_frames],
-            turn_recv.at[stage],
+
+    def send_spectra(k, stage):
+        start = pl.multiple_of(z_lo * frames + k * chunk, chunk)
+        target = held.at[stage, :, my_rows, pl.ds(start, chunk)]
+        pltpu.make_async_copy(
+            spec.at[k, stage, af * 2 + z_lo], target, turn_recv.at[stage]
         ).start()
 
         @pl.loop(1, PEERS)
         def _(step):
             to_af, to_ta, to_lo = turn_peer(step)
             pltpu.make_async_remote_copy(
-                src_ref=spec_ref.at[stage, to_af * 2 + to_lo],
-                dst_ref=held.at[stage, :, my_rows, my_frames],
+                src_ref=spec.at[k, stage, to_af * 2 + to_lo],
+                dst_ref=target,
                 send_sem=turn_send.at[stage],
                 recv_sem=turn_recv.at[stage],
                 device_id={"af": to_af, "ta": to_ta},
                 device_id_type=MESH,
             ).start()
+
+    def channelize(first, count):
+        base = lax.div(first, chunk) * chunk
+
+        @pl.loop(0, count)
+        def _(step):
+            f0 = first + (count - 1 - step) * BLOCK
+            for lane in range(samp_len // 128):
+                cols = pl.ds(lane * 128, 128)
+                taps = [
+                    jnp.broadcast_to(window[pl.ds(p, 1), cols], (inputs, 128))
+                    for p in range(TAPS)
+                ]
+                recent = [samples[f0 + p, :, cols].astype(jnp.float32) for p in range(edge)]
+                for f in range(BLOCK):
+                    recent.append(samples[f0 + f + edge, :, cols].astype(jnp.float32))
+                    acc = taps[0] * recent[0]
+                    for p in range(1, TAPS):
+                        acc = acc + taps[p] * recent[p]
+                    filtered[pl.ds(f * inputs, inputs), cols] = acc.astype(jnp.bfloat16)
+                    recent = recent[1:]
+            block = jnp.dot(filtered[...], table[...], preferred_element_type=jnp.float32)
+            at = pl.ds(pl.multiple_of((f0 - base) * inputs, BLOCK * inputs), BLOCK * inputs)
+            for stage in range(STAGES):
+                spectra[stage, at, :] = block[:, stage * 128 : (stage + 1) * 128]
+
+    def arrange(k, stage):
+        for i in range(inputs):
+            by_frame = spectra[stage, pl.ds(i, chunk, stride=inputs), :]
+            turned[pl.ds(i, 128, stride=inputs), :] = by_frame.T
+        pieces = turned[...].astype(jnp.bfloat16)
+        spec[k, stage] = pieces.reshape(spec.shape[2:])
+
+    for load in loads[:3]:
+        load.wait()
+    per_chunk = chunk // BLOCK
+    channelize(chunk, per_chunk)
+    arrange(1, 0)
+
+    pl.semaphore_wait(barrier, n_greet)
+    ahead = pltpu.make_async_remote_copy(
+        src_ref=x_hbm.at[pl.ds(frames - edge, edge)],
+        dst_ref=halo,
+        send_sem=halo_send,
+        recv_sem=halo_recv,
+        device_id={"af": af, "ta": after},
+        device_id_type=MESH,
+    )
+    ahead.start()
+    send_spectra(1, 0)
+    arrange(1, 1)
+
+    loads[3].wait()
+    channelize(BLOCK, per_chunk - 1)
+    ahead.wait()
+    samples[pl.ds(0, edge)] = jnp.where(ta > 0, halo[...], jnp.zeros_like(halo))
+    channelize(0, 1)
+    arrange(0, 0)
+    send_spectra(0, 0)
+    send_spectra(1, 1)
+    arrange(0, 1)
+    send_spectra(0, 1)
 
     nt = (((1,), (1,)), ((), ()))
 
@@ -183,7 +275,7 @@
         out_ref[:, k, :] = finals[k]
 
     for stage in range(STAGES):
-        sent = spec_ref.at[stage, pl.ds(0, PEERS - 1)]
+        sent = spec.at[:, stage, pl.ds(0, PEERS - 1)]
         pltpu.make_async_copy(sent, sent, turn_send.at[stage]).wait()
         sent = gathered.at[stage, pl.ds(0, NY - 1)]
         pltpu.make_async_copy(sent, sent, row_send.at[stage]).wait()
@@ -191,60 +283,43 @@
         pltpu.make_async_copy(sent, sent, swap_send.at[stage]).wait()
 
 
-def correlate(spectrum):
-    _, _, _, inputs, frames = spectrum.shape
+def on_device(samples):
+    frames, inputs, samp_len = samples.shape
     all_inputs = inputs * lax.axis_size("af")
     rows = all_inputs // NY
+    chunk = frames // CHUNKS
+    window = jnp.asarray(tap_window(TAPS, samp_len))
+    table = jnp.asarray(dft_table(samp_len, CH))
+    f32, bf16 = jnp.float32, jnp.bfloat16
     dma = pltpu.SemaphoreType.DMA
+    anywhere = pl.BlockSpec(memory_space=pltpu.HBM)
     return pl.pallas_call(
         correlate_kernel,
-        out_shape=jax.ShapeDtypeStruct((rows // 2, 2 * STAGES, all_inputs), jnp.float32),
-        in_specs=[pl.BlockSpec(memory_space=pltpu.VMEM)],
+        out_shape=jax.ShapeDtypeStruct((rows // 2, 2 * STAGES, all_inputs), f32),
+        in_specs=[anywhere] * 3,
         out_specs=pl.BlockSpec(memory_space=pltpu.VMEM),
         scratch_shapes=[
-            pltpu.VMEM((STAGES, 2, all_inputs, 2 * frames), jnp.bfloat16),
-            pltpu.VMEM((STAGES, all_inputs, all_inputs), jnp.bfloat16),
-            pltpu.VMEM((STAGES, NY, rows, all_inputs), jnp.bfloat16),
-            pltpu.VMEM((STAGES, rows, all_inputs), jnp.float32),
-            pltpu.VMEM((2 * STAGES, rows // 2, all_inputs), jnp.float32),
+            pltpu.VMEM(window.shape, f32),
+            pltpu.VMEM(table.shape, bf16),
+            pltpu.VMEM((frames + TAPS - 1, inputs, samp_len), bf16),
+            pltpu.VMEM((TAPS - 1, inputs, samp_len), bf16),
+            pltpu.VMEM((BLOCK * inputs, samp_len), bf16),
+            pltpu.VMEM((STAGES, chunk * inputs, 128), f32),
+            pltpu.VMEM((128 * inputs, chunk), f32),
+            pltpu.VMEM((CHUNKS, STAGES, PEERS, 2, inputs, chunk), bf16),
+            pltpu.VMEM((STAGES, 2, all_inputs, 2 * frames), bf16),
+            pltpu.VMEM((STAGES, all_inputs, all_inputs), bf16),
+            pltpu.VMEM((STAGES, NY, rows, all_inputs), bf16),
+            pltpu.VMEM((STAGES, rows, all_inputs), f32),
+            pltpu.VMEM((2 * STAGES, rows // 2, all_inputs), f32),
+            dma((4,)), dma, dma,
             dma((STAGES,)), dma((STAGES,)), dma((STAGES,)),
             dma((STAGES,)), dma((STAGES,)), dma((STAGES,)),
         ],
         compiler_params=pltpu.CompilerParams(
-            collective_id=0, has_side_effects=True, vmem_limit_bytes=48 * 2**20
+            collective_id=0, has_side_effects=True, vmem_limit_bytes=67_000_000
         ),
-    )(spectrum)
-
-
-def passed_along(value, axis, steps):
-    count = lax.axis_size(axis)
-    first, last = (max(0, -steps), min(count, count - steps))
-    return lax.ppermute(value, axis, [(source, source + steps) for source in range(first, last)])
-
-
-def filtered_by(weights, extended, frames):
-    total = jnp.zeros((frames,) + extended.shape[1:], jnp.float32)
-    for tap in range(TAPS):
-        total = total + weights[tap][None, None, :] * extended[tap : tap + frames].astype(
-            jnp.float32
-        )
-    return total.astype(jnp.bfloat16)
-
-
-def on_device(samples):
-    frames, inputs, samp_len = samples.shape
-    weights = jnp.asarray(tap_window(TAPS, samp_len))
-    halo = TAPS - 1
-    earlier = passed_along(samples[frames - halo :], "ta", 1)
-    padded = jnp.pad(samples, ((halo, 0), (0, 0), (0, 0)))
-    filtered = filtered_by(weights, padded, frames)
-    first = filtered_by(weights, jnp.concatenate([earlier, samples[:halo]], axis=0), halo)
-    filtered = lax.dynamic_update_slice(filtered, first, (0, 0, 0))
-    table = jnp.asarray(dft_table(samp_len, CH))
-    spectrum = jnp.einsum("nc,fin->cif", table, filtered, preferred_element_type=jnp.float32)
-    spectrum = spectrum.astype(jnp.bfloat16)
-    spectrum = spectrum.reshape(STAGES, PEERS, 2, inputs, frames)
-    return correlate(spectrum)
+    )(samples, window, table)
 
 
 def solution(mesh):

time: 102 us -> 85.7 us (0.84)
  the two profiles are of different devices: /device:TPU:56 before, /device:TPU:16 now
where the time goes in v2:
time: 85.7 us; the launch traced here: 85.6 us
  Pallas kernels  83.9 us (98%)
  local copies, waits for them, and re-layouts  1.67 us (2%)
    pallas_call x1, Pallas kernels, on_device(): pl.pallas_call(correlate_kernel, out_shape=jax.ShapeDtypeStruct((rows //...  83.9 us

profile of v2, /device:TPU:16, one launch (start us, length us, event | category | flops | bytes accessed | tf_op | source)
XLA Modules:
  0.0 85.6 jit_solution(10761925333649877091)
XLA Ops:
  0.0 83.9 %shard_map.37 = f32[32,4,512]{2,1,0:T(4,128)} custom-call(bf16[256,16,512]{2,1,0:T(8,128)(2,1)} %x_hbm.1, f32[4,512]{1,0:T(4,128)} %constant.4.clone.w_hbm, bf16[512,256]{1,0:T(8,128)(2,1)} %constant.5.clone.t_hbm), custom_call_target="tpu_custom_call" | custom-call | tf_op jit(solution)/shard_map/pallas_call | solution.py:296
  83.9 1.7 %copy.5 = f32[32,4,512]{2,1,0:T(4,128)} copy(f32[32,4,512]{2,1,0:T(4,128)} %shard_map.37) | data formatting | bytes 524288

commit v3 on v2

--- a/solution.py
+++ b/solution.py
@@ -13,7 +13,8 @@
 TAPS = 4
 MESH = pl.DeviceIdType.MESH
 NX, NZ, NY, NCORE = 4, 8, 8, 2
-PEERS = NX * NZ * NCORE
+CHIPS = NX * NZ
+PEERS = CHIPS * NCORE
 STAGES = 2
 CHUNKS = 2
 BLOCK = 16
@@ -44,14 +45,12 @@
     return z, lax.rem(lax.div(af, 2), NX), lax.rem(af, 2), lax.div(ta, 2)
 
 
-def turn_peer(step):
-    z, x, core, y = place()
-    turn, rest = lax.rem(step, NZ), lax.div(step, NZ)
+def turn_peer(turn, along_x, core):
+    z, x, _, y = place()
     odd = lax.rem(turn, 2)
     hop = lax.div(turn + 1, 2)
     z = lax.rem(z + odd * hop + (1 - odd) * (NZ - hop), NZ)
-    x = lax.rem(x + lax.div(rest, NCORE), NX)
-    core = lax.rem(core + rest, NCORE)
+    x = lax.rem(x + along_x, NX)
     z_lo = lax.rem(z, 2)
     return lax.div(z, 2) * 8 + x * 2 + core, y * 2 + z_lo, z_lo
 
@@ -74,22 +73,24 @@
     rows = all_inputs // NY
     half = rows // 2
 
-    loads = [
-        pltpu.make_async_copy(w_hbm, window, load_sem.at[0]),
-        pltpu.make_async_copy(t_hbm, table, load_sem.at[1]),
-        pltpu.make_async_copy(
-            x_hbm.at[pl.ds(chunk - edge, chunk + edge)],
-            samples.at[pl.ds(chunk, chunk + edge)],
-            load_sem.at[2],
-        ),
-        pltpu.make_async_copy(
-            x_hbm.at[pl.ds(0, chunk - edge)],
-            samples.at[pl.ds(edge, chunk - edge)],
-            load_sem.at[3],
-        ),
-    ]
-    for load in loads:
-        load.start()
+    window_load = pltpu.make_async_copy(w_hbm, window, load_sem.at[0])
+    table_load = pltpu.make_async_copy(t_hbm, table, load_sem.at[1])
+
+    def load(first, count, sem):
+        return pltpu.make_async_copy(
+            x_hbm.at[pl.ds(first, count)],
+            samples.at[pl.ds(first + edge, count)],
+            load_sem.at[sem],
+        )
+
+    window_load.start()
+    load(chunk - edge, edge, 2).start()
+    per_chunk = chunk // BLOCK
+    load(chunk, BLOCK, 4).start()
+    table_load.start()
+    for step in range(1, per_chunk):
+        load(chunk + step * BLOCK, BLOCK, 4 + step).start()
+    load(0, chunk - edge, 3).start()
 
     barrier = pltpu.get_barrier_semaphore()
 
@@ -98,10 +99,18 @@
             barrier, inc=1, device_id={"af": to_af, "ta": to_ta}, device_id_type=MESH
         )
 
-    @pl.loop(1, PEERS)
+    @pl.loop(0, (NZ - 1) * NX)
     def _(step):
-        to_af, to_ta, _ = turn_peer(step)
-        greet(to_af, to_ta)
+        for to_core in range(NCORE):
+            along_x = lax.rem(6 - lax.rem(step, NX), NX)
+            to_af, to_ta, _ = turn_peer(NZ - 1 - lax.div(step, NX), along_x, to_core)
+            greet(to_af, to_ta)
+
+    for along_x in (2, 1, 3):
+        for to_core in range(NCORE):
+            to_af, to_ta, _ = turn_peer(0, along_x, to_core)
+            greet(to_af, to_ta)
+    greet(af + 1 - 2 * core, ta)
 
     @pl.loop(1, NY)
     def _(step):
@@ -114,18 +123,15 @@
 
     my_rows = pl.ds(pl.multiple_of(af * inputs, inputs), inputs)
 
-    def send_spectra(k, stage):
-        start = pl.multiple_of(z_lo * frames + k * chunk, chunk)
-        target = held.at[stage, :, my_rows, pl.ds(start, chunk)]
-        pltpu.make_async_copy(
-            spec.at[k, stage, af * 2 + z_lo], target, turn_recv.at[stage]
-        ).start()
-
-        @pl.loop(1, PEERS)
-        def _(step):
-            to_af, to_ta, to_lo = turn_peer(step)
+    def send_spectra(stage, to_core, first, count):
+        lanes = pl.ds(first, count)
+        start = pl.multiple_of(z_lo * frames + first, chunk)
+        target = held.at[stage, :, my_rows, pl.ds(start, count)]
+
+        def send(step):
+            to_af, to_ta, to_lo = turn_peer(lax.rem(step, NZ), lax.div(step, NZ), to_core)
             pltpu.make_async_remote_copy(
-                src_ref=spec.at[k, stage, to_af * 2 + to_lo],
+                src_ref=spec.at[stage, to_af * 2 + to_lo, :, :, lanes],
                 dst_ref=target,
                 send_sem=turn_send.at[stage],
                 recv_sem=turn_recv.at[stage],
@@ -133,12 +139,28 @@
                 device_id_type=MESH,
             ).start()
 
-    def channelize(first, count):
-        base = lax.div(first, chunk) * chunk
+        pl.loop(1, CHIPS)(send)
+
+        @pl.when(core != to_core)
+        def _():
+            send(0)
+
+        @pl.when(core == to_core)
+        def _():
+            pltpu.make_async_copy(
+                spec.at[stage, af * 2 + z_lo, :, :, lanes], target, turn_recv.at[stage]
+            ).start()
+
+    def channelize(first, count, arriving=False):
+        base = first // chunk * chunk
 
         @pl.loop(0, count)
         def _(step):
-            f0 = first + (count - 1 - step) * BLOCK
+            if arriving:
+                f0 = first + step * BLOCK
+                load(0, BLOCK, 4 + step).wait()
+            else:
+                f0 = first + (count - 1 - step) * BLOCK
             for lane in range(samp_len // 128):
                 cols = pl.ds(lane * 128, 128)
                 taps = [
@@ -163,12 +185,12 @@
             by_frame = spectra[stage, pl.ds(i, chunk, stride=inputs), :]
             turned[pl.ds(i, 128, stride=inputs), :] = by_frame.T
         pieces = turned[...].astype(jnp.bfloat16)
-        spec[k, stage] = pieces.reshape(spec.shape[2:])
-
-    for load in loads[:3]:
-        load.wait()
-    per_chunk = chunk // BLOCK
-    channelize(chunk, per_chunk)
+        spec[stage, :, :, :, pl.ds(k * chunk, chunk)] = pieces.reshape(PEERS, 2, inputs, chunk)
+
+    window_load.wait()
+    load(chunk - edge, edge, 2).wait()
+    table_load.wait()
+    channelize(chunk, per_chunk, arriving=True)
     arrange(1, 0)
 
     pl.semaphore_wait(barrier, n_greet)
@@ -181,19 +203,21 @@
         device_id_type=MESH,
     )
     ahead.start()
-    send_spectra(1, 0)
+    send_spectra(0, 0, chunk, chunk)
+    send_spectra(0, 1, chunk, chunk)
     arrange(1, 1)
 
-    loads[3].wait()
+    load(0, chunk - edge, 3).wait()
     channelize(BLOCK, per_chunk - 1)
     ahead.wait()
     samples[pl.ds(0, edge)] = jnp.where(ta > 0, halo[...], jnp.zeros_like(halo))
     channelize(0, 1)
     arrange(0, 0)
-    send_spectra(0, 0)
-    send_spectra(1, 1)
+    send_spectra(0, 0, 0, chunk)
+    send_spectra(0, 1, 0, chunk)
     arrange(0, 1)
-    send_spectra(0, 1)
+    send_spectra(1, 0, 0, frames)
+    send_spectra(1, 1, 0, frames)
 
     nt = (((1,), (1,)), ((), ()))
 
@@ -206,27 +230,26 @@
     upper = row_idx <= col_idx
     lo, hi = pl.ds(0, side), pl.ds(side, side)
 
-    def send_rows(stage, first, last):
-        @pl.loop(first, last)
-        def _(to_y):
+    def send_rows(stage):
+        @pl.loop(0, NY - 1)
+        def _(step):
+            odd = lax.rem(step, 2)
+            hop = NY // 2 - lax.div(step + 1, 2)
+            to_y = lax.rem(y + odd * hop + (1 - odd) * (NY - hop), NY)
             block = pl.ds(pl.multiple_of(to_y * rows, rows), rows)
-
-            @pl.when(to_y != y)
-            def _():
-                pltpu.make_async_remote_copy(
-                    src_ref=part.at[stage, block],
-                    dst_ref=gathered.at[stage, y],
-                    send_sem=row_send.at[stage],
-                    recv_sem=row_recv.at[stage],
-                    device_id={"af": af, "ta": to_y * 2 + z_lo},
-                    device_id_type=MESH,
-                ).start()
-
-            @pl.when(to_y == y)
-            def _():
-                pltpu.make_async_copy(
-                    part.at[stage, block], gathered.at[stage, y], row_recv.at[stage]
-                ).start()
+            pltpu.make_async_remote_copy(
+                src_ref=part.at[stage, block],
+                dst_ref=gathered.at[stage, y],
+                send_sem=row_send.at[stage],
+                recv_sem=row_recv.at[stage],
+                device_id={"af": af, "ta": to_y * 2 + z_lo},
+                device_id_type=MESH,
+            ).start()
+
+        own = pl.ds(pl.multiple_of(y * rows, rows), rows)
+        pltpu.make_async_copy(
+            part.at[stage, own], gathered.at[stage, y], row_recv.at[stage]
+        ).start()
 
     for stage in range(STAGES):
         pltpu.make_async_copy(held.at[stage], held.at[stage], turn_recv.at[stage]).wait()
@@ -238,10 +261,9 @@
             part[stage, own, own] = jnp.where(upper, real, imag).astype(part.dtype)
             if own is lo:
                 part[stage, own, other] = (dot(a, c) + dot(b, d)).astype(part.dtype)
-                send_rows(stage, 0, NY // 2)
             else:
                 part[stage, own, other] = (dot(b, c) - dot(a, d)).astype(part.dtype)
-                send_rows(stage, NY // 2, NY)
+                send_rows(stage)
 
     scale = 1.0 / (frames * lax.axis_size("ta"))
     own_half = pl.ds(pl.multiple_of(z_lo * half, half), half)
@@ -275,7 +297,7 @@
         out_ref[:, k, :] = finals[k]
 
     for stage in range(STAGES):
-        sent = spec.at[:, stage, pl.ds(0, PEERS - 1)]
+        sent = spec.at[stage, pl.ds(0, PEERS - 1)]
         pltpu.make_async_copy(sent, sent, turn_send.at[stage]).wait()
         sent = gathered.at[stage, pl.ds(0, NY - 1)]
         pltpu.make_async_copy(sent, sent, row_send.at[stage]).wait()
@@ -306,13 +328,13 @@
             pltpu.VMEM((BLOCK * inputs, samp_len), bf16),
             pltpu.VMEM((STAGES, chunk * inputs, 128), f32),
             pltpu.VMEM((128 * inputs, chunk), f32),
-            pltpu.VMEM((CHUNKS, STAGES, PEERS, 2, inputs, chunk), bf16),
+            pltpu.VMEM((STAGES, PEERS, 2, inputs, frames), bf16),
             pltpu.VMEM((STAGES, 2, all_inputs, 2 * frames), bf16),
             pltpu.VMEM((STAGES, all_inputs, all_inputs), bf16),
             pltpu.VMEM((STAGES, NY, rows, all_inputs), bf16),
             pltpu.VMEM((STAGES, rows, all_inputs), f32),
             pltpu.VMEM((2 * STAGES, rows // 2, all_inputs), f32),
-            dma((4,)), dma, dma,
+            dma((4 + chunk // BLOCK,)), dma, dma,
             dma((STAGES,)), dma((STAGES,)), dma((STAGES,)),
             dma((STAGES,)), dma((STAGES,)), dma((STAGES,)),
         ],

time: 85.7 us -> 79.5 us (0.928)
  the two profiles are of different devices: /device:TPU:16 before, /device:TPU:1 now
where the time goes in v3:
time: 79.5 us; the launch traced here: 79.4 us
  Pallas kernels  77.7 us (98%)
  local copies, waits for them, and re-layouts  1.67 us (2%)
    pallas_call x1, Pallas kernels, on_device(): pl.pallas_call(correlate_kernel, out_shape=jax.ShapeDtypeStruct((rows //...  77.7 us
    unnamed x1, local copies, waits for them, and re-layouts  1.67 us

profile of v3, /device:TPU:1, one launch (start us, length us, event | category | flops | bytes accessed | tf_op | source)
XLA Modules:
  0.0 79.4 jit_solution(14241506914744105473)
XLA Ops:
  0.0 77.7 %shard_map.37 = f32[32,4,512]{2,1,0:T(4,128)} custom-call(bf16[256,16,512]{2,1,0:T(8,128)(2,1)} %x_hbm.1, f32[4,512]{1,0:T(4,128)} %constant.4.clone.w_hbm, bf16[512,256]{1,0:T(8,128)(2,1)} %constant.5.clone.t_hbm), custom_call_target="tpu_custom_call" | custom-call | tf_op jit(solution)/shard_map/pallas_call | solution.py:318
  77.7 1.7 %copy.5 = f32[32,4,512]{2,1,0:T(4,128)} copy(f32[32,4,512]{2,1,0:T(4,128)} %shard_map.37) | data formatting | bytes 524288

commit v4 on v3

--- a/solution.py
+++ b/solution.py
@@ -13,6 +13,8 @@
 TAPS = 4
 MESH = pl.DeviceIdType.MESH
 NX, NZ, NY, NCORE = 4, 8, 8, 2
+N_ZHI = NZ // 2
+NEAR, FAR = (0, 1, 3), 2
 CHIPS = NX * NZ
 PEERS = CHIPS * NCORE
 STAGES = 2
@@ -121,35 +123,44 @@
     greet(af, before)
     n_greet = PEERS - 1 + NY - 1 + 2
 
-    my_rows = pl.ds(pl.multiple_of(af * inputs, inputs), inputs)
+    my_slot = (x * N_ZHI + lax.div(z, 2)) * NCORE + core
+    my_rows = pl.ds(pl.multiple_of(my_slot * inputs, inputs), inputs)
 
     def send_spectra(stage, to_core, first, count):
         lanes = pl.ds(first, count)
         start = pl.multiple_of(z_lo * frames + first, chunk)
         target = held.at[stage, :, my_rows, pl.ds(start, count)]
-
-        def send(step):
-            to_af, to_ta, to_lo = turn_peer(lax.rem(step, NZ), lax.div(step, NZ), to_core)
+        far_sem = turn_recv.at[STAGES if stage == STAGES - 1 else stage]
+
+        def send(step, along_x, recv_sem):
+            to_af, to_ta, to_lo = turn_peer(step, along_x, to_core)
             pltpu.make_async_remote_copy(
                 src_ref=spec.at[stage, to_af * 2 + to_lo, :, :, lanes],
                 dst_ref=target,
                 send_sem=turn_send.at[stage],
-                recv_sem=turn_recv.at[stage],
+                recv_sem=recv_sem,
                 device_id={"af": to_af, "ta": to_ta},
                 device_id_type=MESH,
             ).start()
 
-        pl.loop(1, CHIPS)(send)
+        @pl.loop(1, len(NEAR) * NZ)
+        def _(step):
+            group = lax.div(step, NZ)
+            send(lax.rem(step, NZ), group + lax.div(group, 2), turn_recv.at[stage])
 
         @pl.when(core != to_core)
         def _():
-            send(0)
+            send(0, 0, turn_recv.at[stage])
 
         @pl.when(core == to_core)
         def _():
             pltpu.make_async_copy(
                 spec.at[stage, af * 2 + z_lo, :, :, lanes], target, turn_recv.at[stage]
             ).start()
+
+        @pl.loop(0, NZ)
+        def _(step):
+            send(step, FAR, far_sem)
 
     def channelize(first, count, arriving=False):
         base = first // chunk * chunk
@@ -224,84 +235,152 @@
     def dot(a, b):
         return lax.dot_general(a, b, nt, preferred_element_type=jnp.float32)
 
-    side = all_inputs // 2
-    row_idx = lax.broadcasted_iota(jnp.int32, (side, side), 0)
-    col_idx = lax.broadcasted_iota(jnp.int32, (side, side), 1)
-    upper = row_idx <= col_idx
-    lo, hi = pl.ds(0, side), pl.ds(side, side)
-
-    def send_rows(stage):
-        @pl.loop(0, NY - 1)
-        def _(step):
-            odd = lax.rem(step, 2)
-            hop = NY // 2 - lax.div(step + 1, 2)
-            to_y = lax.rem(y + odd * hop + (1 - odd) * (NY - hop), NY)
-            block = pl.ds(pl.multiple_of(to_y * rows, rows), rows)
+    group = all_inputs // NX
+    gap = lax.broadcasted_iota(jnp.int32, (half, group), 0)
+    lane = lax.broadcasted_iota(jnp.int32, (half, group), 1)
+    gap = gap - (lane // half * group + lane % half)
+
+    def products(stage, row_groups, col_groups):
+        def rows_of(groups, half_of):
+            starts = [pl.multiple_of(g * group, group) for g in groups]
+            return jnp.concatenate([held[stage, half_of, pl.ds(g, group)] for g in starts], axis=0)
+
+        a, b = (rows_of(row_groups, k) for k in range(2))
+        c, d = (rows_of(col_groups, k) for k in range(2))
+        return dot(a, c) + dot(b, d), dot(b, c) - dot(a, d)
+
+    def pack(stage, row_groups, col_groups, at, real, imag):
+        for m, row_group in enumerate(row_groups):
+            for block in range(N_ZHI):
+                r0 = m * group + block * half
+                for n, col_group in enumerate(col_groups):
+                    upper = gap <= half * (col_group - row_group) - block * group
+                    here = (slice(r0, r0 + half), slice(n * group, (n + 1) * group))
+                    lanes = pl.ds((at + n) * group, group)
+                    part[stage, row_group, block, :, lanes] = jnp.where(
+                        upper, real[here], imag[here]
+                    ).astype(part.dtype)
+
+    def send_rows(stage, to_y, source, target):
+        @pl.when(to_y != y)
+        def _():
             pltpu.make_async_remote_copy(
-                src_ref=part.at[stage, block],
-                dst_ref=gathered.at[stage, y],
+                src_ref=source,
+                dst_ref=target,
                 send_sem=row_send.at[stage],
                 recv_sem=row_recv.at[stage],
                 device_id={"af": af, "ta": to_y * 2 + z_lo},
                 device_id_type=MESH,
             ).start()
 
-        own = pl.ds(pl.multiple_of(y * rows, rows), rows)
-        pltpu.make_async_copy(
-            part.at[stage, own], gathered.at[stage, y], row_recv.at[stage]
-        ).start()
-
-    for stage in range(STAGES):
-        pltpu.make_async_copy(held.at[stage], held.at[stage], turn_recv.at[stage]).wait()
-        for own, other in ((lo, hi), (hi, lo)):
-            a, b = held[stage, 0, own], held[stage, 1, own]
-            c, d = held[stage, 0, other], held[stage, 1, other]
-            real = dot(a, a) + dot(b, b)
-            imag = dot(b, a) - dot(a, b)
-            part[stage, own, own] = jnp.where(upper, real, imag).astype(part.dtype)
-            if own is lo:
-                part[stage, own, other] = (dot(a, c) + dot(b, d)).astype(part.dtype)
-            else:
-                part[stage, own, other] = (dot(b, c) - dot(a, d)).astype(part.dtype)
-                send_rows(stage)
-
-    scale = 1.0 / (frames * lax.axis_size("ta"))
-    own_half = pl.ds(pl.multiple_of(z_lo * half, half), half)
-    other_half = pl.ds(pl.multiple_of((1 - z_lo) * half, half), half)
-    for stage in range(STAGES):
+        @pl.when(to_y == y)
+        def _():
+            pltpu.make_async_copy(source, target, row_recv.at[stage]).start()
+
+    def send_groups(stage, pieces):
+        @pl.loop(0, N_ZHI)
+        def _(step):
+            late = lax.div(step, 2)
+            ahead = (1 - late) * (2 + step) + late * (3 - step)
+            block = lax.rem(lax.div(y, 2) + ahead, N_ZHI)
+            for row_group, lanes in pieces:
+                send_rows(
+                    stage,
+                    block * 2 + lax.div(row_group, 2),
+                    part.at[stage, row_group, block, :, lanes],
+                    gathered.at[stage, y, lax.rem(row_group, 2), :, lanes],
+                )
+
+    scale = 1.0 / (frames * n_ta)
+
+    def add_up(stage, place_of):
         pltpu.make_async_copy(
             gathered.at[stage], gathered.at[stage], row_recv.at[stage]
         ).wait()
-        acc = gathered[stage, 0].astype(jnp.float32)
-        for k in range(1, NY):
-            acc = acc + gathered[stage, k].astype(jnp.float32)
-        total[stage] = acc * scale
+        lane_group = lane // half
+
+        def half_sum(part_of):
+            sums = []
+            for g in range(NX):
+                lanes = pl.ds(pl.multiple_of(place_of(g) * group, group), group)
+                acc = gathered[stage, 0, part_of, :, lanes].astype(jnp.float32)
+                for k in range(1, NY):
+                    acc = acc + gathered[stage, k, part_of, :, lanes].astype(jnp.float32)
+                sums.append(acc * scale)
+            for block in range(N_ZHI):
+                tile = sums[0] if block == 0 else pltpu.roll(sums[0], group - block * half, 1)
+                for g in range(1, NX):
+                    shift = (g - block) * half % group
+                    moved = pltpu.roll(sums[g], shift, 1) if shift else sums[g]
+                    tile = jnp.where(lane_group == g, moved, tile)
+                yield pl.ds(block * group, group), tile
+
+        for lanes, tile in half_sum(1 - z_lo):
+            total[stage, :, lanes] = tile
+        slot = z_lo * STAGES + stage
         pltpu.make_async_remote_copy(
-            src_ref=total.at[stage, other_half],
-            dst_ref=finals.at[z_lo * STAGES + stage],
+            src_ref=total.at[stage],
+            dst_ref=finals.at[slot],
             send_sem=swap_send.at[stage],
             recv_sem=swap_recv.at[stage],
             device_id={"af": af, "ta": y * 2 + 1 - z_lo},
             device_id_type=MESH,
         ).start()
-        pltpu.make_async_copy(
-            total.at[stage, own_half],
-            finals.at[z_lo * STAGES + stage],
-            swap_recv.at[stage],
-        ).start()
-
-    for stage in range(STAGES):
-        both = finals.at[pl.ds(0, 2)]
-        pltpu.make_async_copy(both, both, swap_recv.at[stage]).wait()
-    for k in range(2 * STAGES):
-        out_ref[:, k, :] = finals[k]
+        for lanes, tile in half_sum(z_lo):
+            finals[slot, :, lanes] = tile
+
+    def finish(stage):
+        pltpu.make_async_copy(finals.at[0], finals.at[0], swap_recv.at[stage]).wait()
+        for k in (stage, STAGES + stage):
+            out_ref[:, k, :] = finals[k]
+
+    pltpu.make_async_copy(held.at[0], held.at[0], turn_recv.at[0]).wait()
+    every = tuple(range(NX))
+    for row_groups in (every[: NX // 2], every[NX // 2 :]):
+        pack(0, row_groups, every, 0, *products(0, row_groups, every))
+
+    @pl.loop(0, NY)
+    def _(step):
+        odd = lax.rem(step, 2)
+        hop = NY // 2 - lax.div(step + 1, 2)
+        to_y = lax.rem(y + odd * hop + (1 - odd) * (NY - hop), NY)
+        source = part.at[0, pl.ds(lax.rem(to_y, 2) * 2, 2), lax.div(to_y, 2)]
+        send_rows(0, to_y, source, gathered.at[0, y])
+
+    near = [lax.rem(x + d, NX) for d in NEAR]
+    far = lax.rem(x + FAR, NX)
+    n_near = len(NEAR)
+    last = STAGES - 1
+    arrived = held.at[last, :, pl.ds(0, n_near * group)]
+    pltpu.make_async_copy(arrived, arrived, turn_recv.at[last]).wait()
+    pack(last, near, near, 0, *products(last, near, near))
+    send_groups(last, [(g, pl.ds(0, n_near * group)) for g in near])
+
+    arrived = held.at[last, :, pl.ds(0, group)]
+    pltpu.make_async_copy(arrived, arrived, turn_recv.at[STAGES]).wait()
+    real, imag = products(last, near + [far], [far])
+    pack(last, [far], near, 0, real[: n_near * group].T, -imag[: n_near * group].T)
+    pack(last, near + [far], [far], n_near, real, imag)
+    pieces = [(g, pl.ds(n_near * group, group)) for g in near]
+    send_groups(last, [(far, pl.ds(0, all_inputs))] + pieces)
+
+    add_up(0, lambda g: g)
+    finish(0)
+
+    def place_of(g):
+        d = lax.rem(g - x + NX, NX)
+        return d + lax.div(d, 2) * (5 - 2 * d)
+
+    add_up(last, place_of)
+
+    finish(last)
 
     for stage in range(STAGES):
         sent = spec.at[stage, pl.ds(0, PEERS - 1)]
         pltpu.make_async_copy(sent, sent, turn_send.at[stage]).wait()
         sent = gathered.at[stage, pl.ds(0, NY - 1)]
         pltpu.make_async_copy(sent, sent, row_send.at[stage]).wait()
-        sent = finals.at[0]
+        sent = total.at[stage]
         pltpu.make_async_copy(sent, sent, swap_send.at[stage]).wait()
 
 
@@ -330,12 +409,12 @@
             pltpu.VMEM((128 * inputs, chunk), f32),
             pltpu.VMEM((STAGES, PEERS, 2, inputs, frames), bf16),
             pltpu.VMEM((STAGES, 2, all_inputs, 2 * frames), bf16),
-            pltpu.VMEM((STAGES, all_inputs, all_inputs), bf16),
-            pltpu.VMEM((STAGES, NY, rows, all_inputs), bf16),
-            pltpu.VMEM((STAGES, rows, all_inputs), f32),
+            pltpu.VMEM((STAGES, NX, N_ZHI, rows // 2, all_inputs), bf16),
+            pltpu.VMEM((STAGES, NY, 2, rows // 2, all_inputs), bf16),
+            pltpu.VMEM((STAGES, rows // 2, all_inputs), f32),
             pltpu.VMEM((2 * STAGES, rows // 2, all_inputs), f32),
             dma((4 + chunk // BLOCK,)), dma, dma,
-            dma((STAGES,)), dma((STAGES,)), dma((STAGES,)),
+            dma((STAGES,)), dma((STAGES + 1,)), dma((STAGES,)),
             dma((STAGES,)), dma((STAGES,)), dma((STAGES,)),
         ],
         compiler_params=pltpu.CompilerParams(

time: 79.5 us -> 78.2 us (0.984)
  Pallas kernels: 77.7 us -> 76.4 us
    pallas_call x1, Pallas kernels: 77.7 us -> 76.4 us  [on_device(): pl.pallas_call(correlate_kernel, out_shape=jax.ShapeDtypeStruct((rows //...]
where the time goes in v4:
time: 78.2 us; the launch traced here: 78.1 us
  Pallas kernels  76.4 us (98%)
  local copies, waits for them, and re-layouts  1.67 us (2%)
    pallas_call x1, Pallas kernels, on_device(): pl.pallas_call(correlate_kernel, out_shape=jax.ShapeDtypeStruct((rows //...  76.4 us
    unnamed x1, local copies, waits for them, and re-layouts  1.67 us

profile of v4, /device:TPU:1, one launch (start us, length us, event | category | flops | bytes accessed | tf_op | source)
XLA Modules:
  0.0 78.1 jit_solution(17823734124376247621)
XLA Ops:
  0.0 76.4 %shard_map.37 = f32[32,4,512]{2,1,0:T(4,128)} custom-call(bf16[256,16,512]{2,1,0:T(8,128)(2,1)} %x_hbm.1, f32[4,512]{1,0:T(4,128)} %constant.4.clone.w_hbm, bf16[512,256]{1,0:T(8,128)(2,1)} %constant.5.clone.t_hbm), custom_call_target="tpu_custom_call" | custom-call | tf_op jit(solution)/shard_map/pallas_call | solution.py:397
  76.4 1.7 %copy.5 = f32[32,4,512]{2,1,0:T(4,128)} copy(f32[32,4,512]{2,1,0:T(4,128)} %shard_map.37) | data formatting | bytes 524288
